TPU v7x, 32 devices: a whole 2x2x4 slice. The times are simulated.
32 devices in a mesh: ctx: 16 (over z, y, x), wsh: 2 (over core).
Axes of the slice: x: 2, y: 2, z: 4, core: 2. Of those that a mesh axis runs over, the one named last changes fastest.
Arguments:
- inputs: float32 [2, 2048, 1024], P('wsh', 'ctx'), may hold values from -6 to 6
- norm_gain1: float32 [1024], replicated, may hold values from 0.5 to 1.5
- mix_in: bfloat16 [1024, 4096], P(('ctx', 'wsh')), may hold values from -1 to 1
- step_proj: bfloat16 [1024, 24], replicated, may hold values from -0.4375 to 0.4375
- conv_weight: float32 [4, 1792], replicated, may hold values from -3 to 3
- conv_bias: float32 [1792], replicated, may hold values from -3 to 3
- step_bias: float32 [24], replicated, may hold values from -1 to 1
- decay_log: float32 [24], replicated, may hold values from -11.5 to -3
- skip_gain: float32 [24], replicated, may hold values from 0.5 to 1.5
- mamba_gain: float32 [1536], replicated, may hold values from 0.5 to 1.5
- mix_out: bfloat16 [2048, 1024], P(('ctx', 'wsh')), may hold values from -0.25 to 0.25
- norm_gain2: float32 [1024], replicated, may hold values from 0.5 to 1.5
- mlp_in: bfloat16 [1024, 4096], P(('ctx', 'wsh')), may hold values from -0.1875 to 0.1875
- mlp_out: bfloat16 [2048, 1024], P(('ctx', 'wsh')), may hold values from -0.125 to 0.125
- out_grad: float32 [2, 2048, 1024], P('wsh', 'ctx'), may hold values from -6 to 6
Outputs:
- outputs: float32 [2, 2048, 1024], P('wsh', 'ctx')
- input_grad: float32 [2, 2048, 1024], P('wsh', 'ctx')
- norm_gain1_grad: float32 [1024], replicated
- mix_in_grad: float32 [1024, 4096], P(('ctx', 'wsh'))
- step_proj_grad: float32 [1024, 24], replicated
- conv_weight_grad: float32 [4, 1792], replicated
- conv_bias_grad: float32 [1792], replicated
- step_bias_grad: float32 [24], replicated
- decay_log_grad: float32 [24], replicated
- skip_gain_grad: float32 [24], replicated
- mamba_gain_grad: float32 [1536], replicated
- mix_out_grad: float32 [2048, 1024], P(('ctx', 'wsh'))
- norm_gain2_grad: float32 [1024], replicated
- mlp_in_grad: float32 [1024, 4096], P(('ctx', 'wsh'))
- mlp_out_grad: float32 [2048, 1024], P(('ctx', 'wsh'))
All inputs are finite; a program needn't handle non-finite values.
Results may differ from a plain program's by a relative error of at most 0.015.
The roundings to bfloat16 on the way count: a program that leaves them out, or rounds other values in their place, can miss the bound.
Values may be sent and summed in bfloat16 or wider, within the bound.
No kernel may reach another device: no remote copies, remote signals or barrier semaphores. Data moves between devices by JAX's collectives and lax.ppermute only.
A program may use at most 320 MiB of HBM per device.

v0:
```python
from functools import partial

import jax
import jax.numpy as jnp
from jax import lax
from jax.sharding import PartitionSpec as P

MHEADS = 24
MHEAD_DIM = 64
STATE = 128
CONV = 4
ATT_HEADS = 8
KV_HEADS = 2
HEAD_DIM = 64
FF = 2048
INNER = 1536
CONV_CH = 1792


EPSILON = 1e-05
ROPE_BASE = 10000.0
NEG_LARGE = -1e30
HIGHEST = lax.Precision.HIGHEST


def with_halo(array, sides, width):
    for axis, dim in sides:
        size, length = (lax.axis_size(axis), array.shape[dim])
        up = [(i, (i + 1) % size) for i in range(size - 1)]
        down = [(j, i) for i, j in up]
        last = lax.slice_in_dim(array, length - width, length, axis=dim)
        leading = lax.slice_in_dim(array, 0, width, axis=dim)
        before = lax.ppermute(last, axis, up)
        after = lax.ppermute(leading, axis, down)
        array = jnp.concatenate([before, array, after], axis=dim)
    return array


def carried_in(array, axis, combine, identity, reverse):
    size, here = (lax.axis_size(axis), lax.axis_index(axis))
    everything = jax.tree.map(lambda part: lax.all_gather(part, axis), array)
    start = jax.tree.map(
        lambda part, zero: jnp.broadcast_to(jnp.asarray(zero, part.dtype), part.shape),
        array,
        identity,
    )

    def hop(k, before):
        at = size - 1 - k if reverse else k
        reached = at > here if reverse else at < here
        new = combine(before, jax.tree.map(lambda part: part[at], everything))
        return jax.tree.map(lambda a, b: jnp.where(reached, a, b), new, before)

    return lax.fori_loop(0, size, hop, start)


def rms_scale(values, gain_vec):
    return (
        values * lax.rsqrt(jnp.mean(values * values, axis=-1, keepdims=True) + EPSILON) * gain_vec
    )


def rope_apply(values, positions):
    half_dim = values.shape[-1] // 2
    frequency = ROPE_BASE ** (-jnp.arange(half_dim, dtype=jnp.float32) / half_dim)
    angles = positions.astype(jnp.float32)[:, None] * frequency[None, :]
    cosine = jnp.cos(angles)[:, None, :]
    sine_v = jnp.sin(angles)[:, None, :]
    first_part = values[..., :half_dim]
    second = values[..., half_dim:]
    return jnp.concatenate(
        [first_part * cosine - second * sine_v, second * cosine + first_part * sine_v], axis=-1
    )


def token_positions(device, dev_count, row_count, row_index):
    half_rows = row_count // 2
    return jnp.where(
        row_index < half_rows,
        device * half_rows + row_index,
        (2 * dev_count - 1 - device) * half_rows + row_index - half_rows,
    )


def conv_silu(padded, conv_weight, conv_bias):
    taps_count = conv_weight.shape[0]
    length = padded.shape[0] - taps_count + 1
    summed = conv_bias[None, :]
    for offset in range(taps_count):
        summed = summed + conv_weight[offset][None, :] * padded[offset : offset + length]
    return jax.nn.silu(summed)


def mixer_inputs(padded, step_raw, conv_weight, conv_bias, step_bias, decay_log):
    conv_act = conv_silu(padded, conv_weight, conv_bias)
    x_heads = conv_act[:, :INNER].reshape(conv_act.shape[0], MHEADS, MHEAD_DIM)
    b_proj = conv_act[:, INNER : INNER + STATE]
    c_proj = conv_act[:, INNER + STATE :]
    step_size = jax.nn.softplus(step_raw + step_bias[None, :])
    decay_rate = -jnp.exp(decay_log)
    return (x_heads, step_size, decay_rate, b_proj, c_proj)


def span_local(x_heads, step_size, decay_rate, b_proj, c_proj, skip_gain):
    length = x_heads.shape[0]
    causal = jnp.arange(length)[:, None] >= jnp.arange(length)[None, :]
    cumulative = jnp.cumsum(step_size * decay_rate[None, :], axis=0)
    log_gap = cumulative[:, None, :] - cumulative[None, :, :]
    causal3 = causal[:, :, None]
    decay_mat = jnp.where(causal3, jnp.exp(jnp.where(causal3, log_gap, 0.0)), 0.0)
    intersection = jnp.dot(c_proj, b_proj.T, precision=HIGHEST)
    weights = decay_mat * intersection[:, :, None] * step_size[None, :, :]
    intra_out = jnp.einsum("tsh,shp->thp", weights, x_heads, precision=HIGHEST)
    local_out = intra_out + skip_gain[None, :, None] * x_heads
    tail_weight = jnp.exp(cumulative[-1][None, :] - cumulative) * step_size
    weighted_x = tail_weight[:, :, None] * x_heads
    fresh_state = jnp.einsum("shp,sn->hpn", weighted_x, b_proj, precision=HIGHEST)
    return (local_out, fresh_state, cumulative)


def carry_term(c_proj, cumulative, state_in):
    return (
        jnp.einsum("tn,hpn->thp", c_proj, state_in, precision=HIGHEST)
        * jnp.exp(cumulative)[:, :, None]
    )


def half_mixer(padded, step_raw, conv_weight, conv_bias, step_bias, decay_log, skip_gain, state_in):
    x_heads, step_size, decay_rate, b_proj, c_proj = mixer_inputs(
        padded, step_raw, conv_weight, conv_bias, step_bias, decay_log
    )
    local_out, fresh_state, cumulative = span_local(
        x_heads, step_size, decay_rate, b_proj, c_proj, skip_gain
    )
    result = local_out + carry_term(c_proj, cumulative, state_in)
    new_state = jnp.exp(cumulative[-1])[:, None, None] * state_in + fresh_state
    return (result.reshape(result.shape[0], INNER), new_state)


def gated_tail(ssm_out, gate_z, mamba_gain):
    return rms_scale(ssm_out * jax.nn.silu(gate_z), mamba_gain)


def chain_combine(earlier, latter):
    return (earlier[0] * latter[0], latter[0][:, None, None] * earlier[1] + latter[1])


def score_block(q_groups, query_pos, key_block, pos_block):
    raw_scores = jnp.einsum(
        "tkgd,skd->kgts", q_groups, key_block, preferred_element_type=jnp.float32
    ) * HEAD_DIM ** (-0.5)
    return jnp.where(
        pos_block[None, None, None, :] <= query_pos[None, None, :, None], raw_scores, NEG_LARGE
    )


def split_blocks(all_keys, all_values, key_pos):
    key_count = all_keys.shape[0]
    block_len = min(2048, key_count)
    blocks = key_count // block_len
    return (
        all_keys.reshape(blocks, block_len, KV_HEADS, HEAD_DIM),
        all_values.reshape(blocks, block_len, KV_HEADS, HEAD_DIM),
        key_pos.reshape(blocks, block_len),
    )


def attention_forward(queries, all_keys, all_values, query_pos, key_pos):
    row_count = queries.shape[0]
    group_size = ATT_HEADS // KV_HEADS
    q_groups = queries.reshape(row_count, KV_HEADS, group_size, HEAD_DIM)
    key_blocks, value_blocks, pos_blocks = split_blocks(all_keys, all_values, key_pos)

    def max_step(carried, block_item):
        running_max, running_sum = carried
        scores = score_block(q_groups, query_pos, block_item[0], block_item[1])
        new_max = jnp.maximum(running_max, jnp.max(scores, axis=-1))
        running_sum = running_sum * jnp.exp(running_max - new_max) + jnp.sum(
            jnp.exp(scores - new_max[..., None]), axis=-1
        )
        return ((new_max, running_sum), None)

    start_max = jnp.full((KV_HEADS, group_size, row_count), NEG_LARGE, jnp.float32)
    (final_max, final_sum), unused = lax.scan(
        max_step, (start_max, jnp.zeros_like(start_max)), (key_blocks, pos_blocks)
    )
    log_total = final_max + jnp.log(final_sum)

    def out_step(weighted, block_item):
        scores = score_block(q_groups, query_pos, block_item[0], block_item[2])
        attn_prob = jnp.exp(scores - log_total[..., None]).astype(jnp.bfloat16)
        return (
            weighted
            + jnp.einsum(
                "kgts,skd->tkgd", attn_prob, block_item[1], preferred_element_type=jnp.float32
            ),
            None,
        )

    start_out = jnp.zeros((row_count, KV_HEADS, group_size, HEAD_DIM), jnp.float32)
    weighted, unused_two = lax.scan(out_step, start_out, (key_blocks, value_blocks, pos_blocks))
    return (weighted.reshape(row_count, ATT_HEADS * HEAD_DIM), log_total)


def attention_backward(
    queries, all_keys, all_values, query_pos, key_pos, log_total, attn_f32, grad_attn
):
    row_count = queries.shape[0]
    key_count = all_keys.shape[0]
    group_size = ATT_HEADS // KV_HEADS
    score_scale = HEAD_DIM ** (-0.5)
    q_groups = queries.reshape(row_count, KV_HEADS, group_size, HEAD_DIM)
    d_groups = grad_attn.reshape(row_count, KV_HEADS, group_size, HEAD_DIM)
    row_dot = jnp.sum(
        (grad_attn.astype(jnp.float32) * attn_f32).reshape(
            row_count, KV_HEADS, group_size, HEAD_DIM
        ),
        axis=-1,
    )
    row_dot = jnp.transpose(row_dot, (1, 2, 0))
    key_blocks, value_blocks, pos_blocks = split_blocks(all_keys, all_values, key_pos)

    def grad_step(grad_q, block_item):
        key_block, value_block, pos_block = block_item
        scores = score_block(q_groups, query_pos, key_block, pos_block)
        attn_prob = jnp.exp(scores - log_total[..., None])
        grad_prob = jnp.einsum(
            "tkgd,skd->kgts", d_groups, value_block, preferred_element_type=jnp.float32
        )
        grad_score = (attn_prob * (grad_prob - row_dot[..., None])).astype(jnp.bfloat16)
        grad_vb = jnp.einsum(
            "kgts,tkgd->skd",
            attn_prob.astype(jnp.bfloat16),
            d_groups,
            preferred_element_type=jnp.float32,
        )
        grad_kb = (
            jnp.einsum("kgts,tkgd->skd", grad_score, q_groups, preferred_element_type=jnp.float32)
            * score_scale
        )
        grad_q = (
            grad_q
            + jnp.einsum(
                "kgts,skd->tkgd", grad_score, key_block, preferred_element_type=jnp.float32
            )
            * score_scale
        )
        return (grad_q, (grad_kb, grad_vb))

    start_q = jnp.zeros((row_count, KV_HEADS, group_size, HEAD_DIM), jnp.float32)
    grad_q, (grad_keys, grad_values) = lax.scan(
        grad_step, start_q, (key_blocks, value_blocks, pos_blocks)
    )
    return (
        grad_q.reshape(row_count, ATT_HEADS, HEAD_DIM),
        grad_keys.reshape(key_count, KV_HEADS * HEAD_DIM),
        grad_values.reshape(key_count, KV_HEADS * HEAD_DIM),
    )


def body(
    inputs,
    norm_gain1,
    mix_in,
    step_proj,
    conv_weight,
    conv_bias,
    step_bias,
    decay_log,
    skip_gain,
    mamba_gain,
    mix_out,
    norm_gain2,
    mlp_in,
    mlp_out,
    out_grad,
):
    residual = inputs[0]
    row_count = residual.shape[0]
    half_rows = row_count // 2
    rim_len = CONV - 1
    q_width = ATT_HEADS * HEAD_DIM
    kv_width = KV_HEADS * HEAD_DIM
    dev_count = lax.axis_size("ctx")
    device = lax.axis_index("ctx")
    is_last = device == dev_count - 1
    local_pos = token_positions(
        device, dev_count, row_count, jnp.arange(row_count, dtype=jnp.int32)
    )
    key_ids = jnp.arange(row_count * dev_count, dtype=jnp.int32)
    key_pos = token_positions(key_ids // row_count, dev_count, row_count, key_ids % row_count)
    full_in, full_out, full_up, full_down = (
        lax.all_gather(mix_in, ("ctx", "wsh"), axis=0, tiled=True),
        lax.all_gather(mix_out, ("ctx", "wsh"), axis=0, tiled=True),
        lax.all_gather(mlp_in, ("ctx", "wsh"), axis=0, tiled=True),
        lax.all_gather(mlp_out, ("ctx", "wsh"), axis=0, tiled=True),
    )
    normed1 = rms_scale(residual, norm_gain1).astype(jnp.bfloat16)
    projected = jnp.dot(normed1, full_in, preferred_element_type=jnp.float32)
    step_raw = jnp.dot(normed1, step_proj, preferred_element_type=jnp.float32)
    gate_z = projected[:, :INNER]
    conv_in = projected[:, INNER : INNER + CONV_CH]
    attn_cols = projected[:, INNER + CONV_CH :]
    q_raw = attn_cols[:, :q_width].reshape(row_count, ATT_HEADS, HEAD_DIM)
    k_raw = attn_cols[:, q_width : q_width + kv_width].reshape(row_count, KV_HEADS, HEAD_DIM)
    v_raw = attn_cols[:, q_width + kv_width :]
    tail_rows = jnp.stack(
        [conv_in[half_rows - rim_len : half_rows], conv_in[row_count - rim_len :]]
    )
    beside_all = with_halo(tail_rows[None], (("ctx", 0),), 1)
    rim_first = beside_all[0, 0]
    rim_second = jnp.where(is_last, tail_rows[0], beside_all[2, 1])
    padded = jnp.stack(
        [
            jnp.concatenate([rim_first, conv_in[:half_rows]], axis=0),
            jnp.concatenate([rim_second, conv_in[half_rows:]], axis=0),
        ]
    )
    step_pair = step_raw.reshape(2, half_rows, MHEADS)

    def local_parts(padded_one, step_one):
        x_heads, step_size, decay_rate, b_proj, c_proj = mixer_inputs(
            padded_one, step_one, conv_weight, conv_bias, step_bias, decay_log
        )
        local_out, fresh_state, cumulative = span_local(
            x_heads, step_size, decay_rate, b_proj, c_proj, skip_gain
        )
        return (local_out, fresh_state, cumulative, c_proj)

    local_out, fresh_state, cumulative, c_proj = jax.vmap(local_parts)(padded, step_pair)
    decays = jnp.exp(cumulative[:, -1])
    identity = (
        jnp.ones((MHEADS,), jnp.float32),
        jnp.zeros((MHEADS, MHEAD_DIM, STATE), jnp.float32),
    )
    rising = carried_in((decays[0], fresh_state[0]), "ctx", chain_combine, identity, False)
    state_first = rising[1]
    end_first = decays[0][:, None, None] * state_first + fresh_state[0]
    lead_second = jnp.where(
        is_last, decays[1][:, None, None] * end_first + fresh_state[1], fresh_state[1]
    )
    falling = carried_in((decays[1], lead_second), "ctx", chain_combine, identity, True)
    state_second = jnp.where(is_last, end_first, falling[1])
    states = jnp.stack([state_first, state_second])
    ssm_out = (local_out + jax.vmap(carry_term)(c_proj, cumulative, states)).reshape(
        row_count, INNER
    )
    mamba_part = gated_tail(ssm_out, gate_z, mamba_gain)
    queries = rope_apply(q_raw, local_pos).astype(jnp.bfloat16)
    keys_local = rope_apply(k_raw, local_pos).reshape(row_count, kv_width).astype(jnp.bfloat16)
    all_keys, all_values = (
        lax.all_gather(keys_local, "ctx", axis=0, tiled=True),
        lax.all_gather(v_raw.astype(jnp.bfloat16), "ctx", axis=0, tiled=True),
    )
    attn_f32, log_total = attention_forward(queries, all_keys, all_values, local_pos, key_pos)
    joined = jnp.concatenate(
        [mamba_part.astype(jnp.bfloat16), attn_f32.astype(jnp.bfloat16)], axis=1
    )
    middle = residual + jnp.dot(joined, full_out, preferred_element_type=jnp.float32)
    normed2 = rms_scale(middle, norm_gain2).astype(jnp.bfloat16)
    up_proj = jnp.dot(normed2, full_up, preferred_element_type=jnp.float32)
    gate_part = up_proj[:, :FF]
    up_part = up_proj[:, FF:]
    activated = (jax.nn.silu(gate_part) * up_part).astype(jnp.bfloat16)
    outputs = middle + jnp.dot(activated, full_down, preferred_element_type=jnp.float32)
    grad_top = out_grad[0]
    grad_top_b = grad_top.astype(jnp.bfloat16)
    down_grad = jnp.dot(activated.T, grad_top_b, preferred_element_type=jnp.float32)
    grad_act = jnp.dot(grad_top_b, full_down.T, preferred_element_type=jnp.float32)
    sigmoid_g = jax.nn.sigmoid(gate_part)
    grad_gate = grad_act * up_part * sigmoid_g * (1.0 + gate_part * (1.0 - sigmoid_g))
    grad_up = grad_act * gate_part * sigmoid_g
    grad_mlp = jnp.concatenate([grad_gate, grad_up], axis=1).astype(jnp.bfloat16)
    up_grad = jnp.dot(normed2.T, grad_mlp, preferred_element_type=jnp.float32)
    grad_normed2 = jnp.dot(grad_mlp, full_up.T, preferred_element_type=jnp.float32)
    unused_two, norm_back2 = jax.vjp(rms_scale, middle, norm_gain2)
    grad_mid_n, gain2_part = norm_back2(grad_normed2)
    grad_middle = grad_top + grad_mid_n
    grad_mid_b = grad_middle.astype(jnp.bfloat16)
    mixout_grad = jnp.dot(joined.T, grad_mid_b, preferred_element_type=jnp.float32)
    grad_joined = jnp.dot(grad_mid_b, full_out.T, preferred_element_type=jnp.float32)
    unused_tail, tail_back = jax.vjp(gated_tail, ssm_out, gate_z, mamba_gain)
    grad_ssm, grad_z, mgain_part = tail_back(grad_joined[:, :INNER])
    grad_attn = grad_joined[:, INNER:].astype(jnp.bfloat16)
    grad_q, grad_keys, grad_values = attention_backward(
        queries, all_keys, all_values, local_pos, key_pos, log_total, attn_f32, grad_attn
    )
    keys_back, values_back = (
        lax.psum_scatter(grad_keys, "ctx", scatter_dimension=0, tiled=True),
        lax.psum_scatter(grad_values, "ctx", scatter_dimension=0, tiled=True),
    )
    unused_q, rope_back_q = jax.vjp(partial(rope_apply, positions=local_pos), q_raw)
    unused_k, rope_back_k = jax.vjp(partial(rope_apply, positions=local_pos), k_raw)
    (grad_q_raw,) = rope_back_q(grad_q)
    (grad_k_raw,) = rope_back_k(keys_back.reshape(row_count, KV_HEADS, HEAD_DIM))
    pair_mixer = jax.vmap(half_mixer, in_axes=(0, 0, None, None, None, None, None, 0))
    unused_m, mixer_back = jax.vjp(
        pair_mixer,
        padded,
        step_pair,
        conv_weight,
        conv_bias,
        step_bias,
        decay_log,
        skip_gain,
        states,
    )
    grad_pair = grad_ssm.reshape(2, half_rows, INNER)
    first_pass = mixer_back((grad_pair, jnp.zeros_like(states)))
    own_grads = first_pass[7]
    back_up = carried_in((decays[1], own_grads[1]), "ctx", chain_combine, identity, False)
    end_second = back_up[1]
    start_second = decays[1][:, None, None] * end_second + own_grads[1]
    lead_first = jnp.where(
        is_last, decays[0][:, None, None] * start_second + own_grads[0], own_grads[0]
    )
    back_down = carried_in((decays[0], lead_first), "ctx", chain_combine, identity, True)
    end_first_g = jnp.where(is_last, start_second, back_down[1])
    second_pass = mixer_back((jnp.zeros_like(grad_pair), jnp.stack([end_first_g, end_second])))
    mixer_grads = jax.tree.map(jnp.add, first_pass, second_pass)
    grad_padded = mixer_grads[0]
    grad_rims = grad_padded[:, :rim_len]
    grad_conv = grad_padded[:, rim_len:].reshape(row_count, CONV_CH)
    moved_rims = with_halo(grad_rims[None], (("ctx", 0),), 1)
    add_first = moved_rims[2, 0] + jnp.where(is_last, grad_rims[1], 0.0)
    grad_conv = grad_conv.at[half_rows - rim_len : half_rows].add(add_first)
    grad_conv = grad_conv.at[row_count - rim_len :].add(moved_rims[0, 1])
    grad_proj = jnp.concatenate(
        [
            grad_z,
            grad_conv,
            grad_q_raw.reshape(row_count, q_width),
            grad_k_raw.reshape(row_count, kv_width),
            values_back,
        ],
        axis=1,
    ).astype(jnp.bfloat16)
    grad_step = mixer_grads[1].reshape(row_count, MHEADS).astype(jnp.bfloat16)
    in_grad = jnp.dot(normed1.T, grad_proj, preferred_element_type=jnp.float32)
    step_grad = jnp.dot(normed1.T, grad_step, preferred_element_type=jnp.float32)
    grad_normed1 = jnp.dot(grad_proj, full_in.T, preferred_element_type=jnp.float32) + jnp.dot(
        grad_step, step_proj.T, preferred_element_type=jnp.float32
    )
    unused_one, norm_back1 = jax.vjp(rms_scale, residual, norm_gain1)
    grad_res_n, gain1_part = norm_back1(grad_normed1)
    input_grad = grad_middle + grad_res_n
    in_shard, out_shard, up_shard, down_shard = (
        lax.psum_scatter(in_grad, ("ctx", "wsh"), scatter_dimension=0, tiled=True),
        lax.psum_scatter(mixout_grad, ("ctx", "wsh"), scatter_dimension=0, tiled=True),
        lax.psum_scatter(up_grad, ("ctx", "wsh"), scatter_dimension=0, tiled=True),
        lax.psum_scatter(down_grad, ("ctx", "wsh"), scatter_dimension=0, tiled=True),
    )
    small_sums = lax.psum(
        (
            gain1_part,
            step_grad,
            mixer_grads[2],
            mixer_grads[3],
            mixer_grads[4],
            mixer_grads[5],
            mixer_grads[6],
            mgain_part,
            gain2_part,
        ),
        ("ctx", "wsh"),
    )
    return (
        outputs[None],
        input_grad[None],
        small_sums[0],
        in_shard,
        small_sums[1],
        small_sums[2],
        small_sums[3],
        small_sums[4],
        small_sums[5],
        small_sums[6],
        small_sums[7],
        out_shard,
        small_sums[8],
        up_shard,
        down_shard,
    )


def solution(mesh):
    return jax.shard_map(
        body,
        mesh=mesh,
        in_specs=(
            P("wsh", "ctx", None),
            P(),
            P(("ctx", "wsh"), None),
            P(),
            P(),
            P(),
            P(),
            P(),
            P(),
            P(),
            P(("ctx", "wsh"), None),
            P(),
            P(("ctx", "wsh"), None),
            P(("ctx", "wsh"), None),
            P("wsh", "ctx", None),
        ),
        out_specs=(
            P("wsh", "ctx", None),
            P("wsh", "ctx", None),
            P(),
            P(("ctx", "wsh"), None),
            P(),
            P(),
            P(),
            P(),
            P(),
            P(),
            P(),
            P(("ctx", "wsh"), None),
            P(),
            P(("ctx", "wsh"), None),
            P(("ctx", "wsh"), None),
        ),
        check_vma=False,
    )
```

profile of v0, /device:TPU:13, one launch (start us, length us, event | category | flops | bytes accessed | tf_op | source)
XLA Modules:
  0.0 1949.0 jit_solution(15304572507129707949)
XLA Ops:
  13.3 76.3 %all-gather.13.cloned.1.call-done = bf16[1024,4096]{1,0:T(8,128)(2,1)} async-done(((bf16[32,4096]{1,0:T(8,128)(2,1)}), bf16[1024,4096]{1,0:T(8,128)(2,1)}) %all-gather.13.cloned.1.call-update) | async-done | bytes 8388624 | tf_op jit(solution)/shard_map/all_gather | solution.py:293
  111.6 22.4 %all-gather.2 = f32[16,1,24]{2,1,0:T(1,128)S(1)} all-gather(f32[1,1,24]{2,1,0:T(1,128)S(1)} %get-tuple-element.805), channel_id=1, replica_groups=mesh['ctx'=16,'wsh'=2] {'ctx'}, dimensions={0}, use_global_device_ids=true | all-gather | bytes 1632 | tf_op jit(solution)/shard_map/all_gather | solution.py:41
  134.0 126.5 %all-gather.15.cloned.1.call-done = f32[16,24,64,128]{3,2,1,0:T(8,128)} async-done(((f32[1,24,64,128]{3,2,1,0:T(8,128)}), f32[16,24,64,128]{3,2,1,0:T(8,128)}) %all-gather.15.cloned.1.call-update) | async-done | bytes 12582928 | tf_op jit(solution)/shard_map/all_gather | solution.py:41
  260.5 21.5 %while.77 = (s32[]{:T(128)}, f32[24,64,128]{2,1,0:T(8,128)S(1)}, s32[]{:T(128)}, f32[16,24]{1,0:T(8,128)S(1)}, f32[16,24,64,128]{3,2,1,0:T(8,128)}, /*index=5*/s32[]{:T(128)}, s32[]{:T(128)}) while((s32[]{:T(128)}, f32[24,64,128]{2,1,0:T(8,128)S(1)}, s32[]{:T(128)}, f32[16,24]{1,0:T(8,128)S(1)}, f32[16,24,64,128]{3,2,1,0:T(8,128)}, ...), condition=%wide.region_3.4_spmd.clone, body=%wide.region_2.3_spmd.clone.sunk | while | flops 786436 | bytes 2359697 | solution.py:54
  288.4 26.9 %all-gather.3 = f32[16,1,24]{2,1,0:T(1,128)} all-gather(f32[1,1,24]{2,1,0:T(1,128)S(1)} %get-tuple-element.804), channel_id=1, replica_groups=mesh['ctx'=16,'wsh'=2] {'ctx'}, dimensions={0}, use_global_device_ids=true | all-gather | bytes 1632 | tf_op jit(solution)/shard_map/all_gather | solution.py:41
  318.0 38.9 %all_gather.50 = bf16[2048,128]{1,0:T(8,128)(2,1)} all-gather(bf16[128,128]{1,0:T(8,128)(2,1)S(1)} %slice.443), channel_id=1, replica_groups=mesh['ctx'=16,'wsh'=2] {'ctx'}, dimensions={0}, use_global_device_ids=true | all-gather | bytes 557056 | tf_op jit(solution)/shard_map/all_gather | solution.py:353
  360.4 45.6 %all_gather.51 = bf16[2048,128]{0,1:T(8,128)(2,1)} all-gather(bf16[128,128]{0,1:T(8,128)(2,1)S(1)} %bitcast.383), channel_id=1, replica_groups=mesh['ctx'=16,'wsh'=2] {'ctx'}, dimensions={0}, use_global_device_ids=true | all-gather | bytes 557056 | tf_op jit(solution)/shard_map/all_gather | solution.py:352
  419.1 33.9 %all-gather.25.cloned.1.call-done = f32[384,64,128]{2,1,0:T(8,128)} async-done(((f32[24,64,128]{2,1,0:T(8,128)}), f32[384,64,128]{2,1,0:T(8,128)}) %all-gather.25.cloned.1.call-update) | async-done | bytes 12582928 | tf_op jit(solution)/shard_map/all_gather | solution.py:41
  453.0 49.3 %while.78 = (s32[]{:T(128)}, f32[24,64,128]{2,1,0:T(8,128)}, s32[]{:T(128)}, f32[16,24]{1,0:T(8,128)}, f32[16,24,64,128]{3,2,1,0:T(8,128)}, /*index=5*/s32[]{:T(128)}, s32[]{:T(128)}, s32[]{:T(128)}, s32[]{:T(128)}) while((s32[]{:T(128)}, f32[24,64,128]{2,1,0:T(8,128)}, s32[]{:T(128)}, f32[16,24]{1,0:T(8,128)}, ...), condition=%wide.region_5.6_spmd.clone, body=%wide.region_4.5_spmd.clone.sunk | while | flops 786440 | bytes 2359759 | solution.py:54
  526.4 70.3 %all-gather.19.cloned.1.call-done = bf16[1024,4096]{1,0:T(8,128)(2,1)} async-done(((bf16[32,4096]{1,0:T(8,128)(2,1)}), bf16[1024,4096]{1,0:T(8,128)(2,1)}) %all-gather.19.cloned.1.call-update) | async-done | bytes 8388624 | tf_op jit(solution)/shard_map/all_gather | solution.py:295
  602.8 56.9 %all-gather.21.cloned.1.call-done = bf16[2048,1024]{1,0:T(8,128)(2,1)} async-done(((bf16[64,1024]{1,0:T(8,128)(2,1)}), bf16[2048,1024]{1,0:T(8,128)(2,1)}) %all-gather.21.cloned.1.call-update) | async-done | bytes 4194320 | tf_op jit(solution)/shard_map/all_gather | solution.py:296
  689.4 6.9 fusion.5
  698.7 131.6 %all-gather.23.cloned.1.call-done = f32[16,24,64,128]{3,2,1,0:T(8,128)} async-done(((f32[1,24,64,128]{3,2,1,0:T(8,128)}), f32[16,24,64,128]{3,2,1,0:T(8,128)}) %all-gather.23.cloned.1.call-update) | async-done | bytes 12582928 | tf_op jit(solution)/shard_map/all_gather | solution.py:41
  830.3 32.1 %while.79 = (s32[]{:T(128)}, f32[24,64,128]{2,1,0:T(8,128)S(1)}, s32[]{:T(128)}, f32[16,24]{1,0:T(8,128)}, f32[16,24,64,128]{3,2,1,0:T(8,128)}, /*index=5*/s32[]{:T(128)}, s32[]{:T(128)}) while((s32[]{:T(128)}, f32[24,64,128]{2,1,0:T(8,128)S(1)}, s32[]{:T(128)}, f32[16,24]{1,0:T(8,128)}, f32[16,24,64,128]{3,2,1,0:T(8,128)}, ...), condition=%wide.region_15.16_spmd.clone, body=%wide.region_14.15_spmd.clone.sunk | while | flops 786436 | bytes 2359697 | solution.py:54
  886.5 9.6 fusion.95
  942.2 118.1 %all-gather.27.cloned.1.call-done = f32[384,64,128]{2,1,0:T(8,128)} async-done(((f32[24,64,128]{2,1,0:T(8,128)}), f32[384,64,128]{2,1,0:T(8,128)}) %all-gather.27.cloned.1.call-update) | async-done | bytes 12582928 | tf_op jit(solution)/shard_map/all_gather | solution.py:41
  1060.3 49.5 %while.80 = (s32[]{:T(128)}, f32[24,64,128]{2,1,0:T(8,128)}, s32[]{:T(128)}, f32[16,24]{1,0:T(8,128)}, f32[16,24,64,128]{3,2,1,0:T(8,128)}, /*index=5*/s32[]{:T(128)}, s32[]{:T(128)}, s32[]{:T(128)}, s32[]{:T(128)}) while((s32[]{:T(128)}, f32[24,64,128]{2,1,0:T(8,128)}, s32[]{:T(128)}, f32[16,24]{1,0:T(8,128)}, ...), condition=%wide.region_17.18_spmd.clone, body=%wide.region_16.17_spmd.clone.sunk | while | flops 786440 | bytes 2359759 | solution.py:54
  1170.0 9.4 fusion.188
  1192.0 45.9 %all-reduce.30 = (f32[1024]{0:T(1024)}, f32[4,1792]{1,0:T(4,128)}, f32[1792]{0:T(1024)}, f32[24]{0:T(128)}, f32[24]{0:T(128)}, /*index=5*/f32[24]{0:T(128)}, f32[1536]{0:T(1024)}, f32[1024]{0:T(1024)}) all-reduce(f32[1024]{0:T(1024)S(1)} %get-tuple-element.674, ...), channel_id=1, replica_groups=mesh['ctx'=16,'wsh'=2] {'ctx','wsh'}, use_global_device_ids=true, to_apply=%region_39.40 | all-reduce | flops 12616 | bytes 100928 | tf_op jit(solution)/shard_map/psum | solution.py:453
  1238.9 21.0 %reduce-scatter.13.cloned.1.call-done = f32[64,1024]{1,0:T(8,128)} async-done(((f32[2048,1024]{1,0:T(8,128)}), f32[64,1024]{1,0:T(8,128)}) %reduce-scatter.13.cloned.1.call-update) | async-done | bytes 262160 | tf_op jit(solution)/shard_map/reduce_scatter | solution.py:449
  1259.9 148.2 %reduce-scatter.17.cloned.1.call-done = f32[64,1024]{1,0:T(8,128)} async-done(((f32[2048,1024]{1,0:T(8,128)}), f32[64,1024]{1,0:T(8,128)}) %reduce-scatter.17.cloned.1.call-update) | async-done | bytes 262160 | tf_op jit(solution)/shard_map/reduce_scatter | solution.py:451
  1408.1 215.6 %reduce-scatter.15.cloned.1.call-done = f32[32,4096]{1,0:T(8,128)} async-done(((f32[1024,4096]{1,0:T(8,128)}), f32[32,4096]{1,0:T(8,128)}) %reduce-scatter.15.cloned.1.call-update) | async-done | bytes 524304 | tf_op jit(solution)/shard_map/reduce_scatter | solution.py:450
  1623.7 128.4 %all-reduce.33.cloned.1.call-done = f32[1024,24]{0,1:T(8,128)} async-done(((f32[1024,24]{0,1:T(8,128)}), f32[1024,24]{0,1:T(8,128)}) %all-reduce.33.cloned.1.call-update) | async-done | bytes 98320 | tf_op jit(solution)/shard_map/psum | solution.py:453
  1752.1 188.6 %reduce-scatter.11.cloned.1.call-done = f32[32,4096]{1,0:T(8,128)} async-done(((f32[1024,4096]{1,0:T(8,128)}), f32[32,4096]{1,0:T(8,128)}) %reduce-scatter.11.cloned.1.call-update) | async-done | bytes 524304 | tf_op jit(solution)/shard_map/reduce_scatter | solution.py:448
  (655 shorter events, 410.7 us)
Async XLA Ops:
  7.2 82.3 %all-gather.13.cloned.1.call-start = ((), (), s32[]{:S(2)}) async-start(), calls=%async_computation.6 | async-start | bytes 8650752 | tf_op jit(solution)/shard_map/all_gather | solution.py:293
  8.0 252.6 %all-gather.15.cloned.1.call-start = ((), (), s32[]{:S(2)}) async-start(), calls=%async_computation.7 | async-start | bytes 13369344 | tf_op jit(solution)/shard_map/all_gather | solution.py:41
  12.2 274.2 %copy-start.50 = (f32[2,64,24]{2,0,1:T(2,128)}, f32[2,64,24]{2,0,1:T(2,128)S(1)}, u32[]{:S(2)}) copy-start(f32[2,64,24]{2,0,1:T(2,128)S(1)} %get-tuple-element.757) | copy-start | bytes 36868
  12.4 274.8 %copy-start.45 = (f32[2,64,24]{2,1,0:T(8,128)}, f32[2,64,24]{2,1,0:T(8,128)S(1)}, u32[]{:S(2)}) copy-start(f32[2,64,24]{2,1,0:T(8,128)S(1)} %reduce_window_sum.30) | copy-start | bytes 36868
  94.3 5.5 collective-permute-start.1
  97.6 5.8 collective-permute-start
  111.0 342.0 %all-gather.25.cloned.1.call-start = ((), (), s32[]{:S(2)}) async-start(), calls=%async_computation.19 | async-start | bytes 13369344 | tf_op jit(solution)/shard_map/all_gather | solution.py:41
  111.6 170.4 %copy-start.123 = (f32[24]{0:T(128)}, f32[24]{0:T(128)S(1)}, u32[]{:S(2)}) copy-start(f32[24]{0:T(128)S(1)} %get-tuple-element.803) | copy-start | bytes 292
  111.6 390.6 %copy-start.126 = (f32[24]{0:T(128)}, f32[24]{0:T(128)S(1)}, u32[]{:S(2)}) copy-start(f32[24]{0:T(128)S(1)} %get-tuple-element.802) | copy-start | bytes 292
  284.6 237.5 %all-gather.17.cloned.1.call-start = ((), (), s32[]{:S(2)}) async-start(), calls=%async_computation.8 | async-start | bytes 4325376 | tf_op jit(solution)/shard_map/all_gather | solution.py:294
  285.2 311.5 %all-gather.19.cloned.1.call-start = ((), (), s32[]{:S(2)}) async-start(), calls=%async_computation.9 | async-start | bytes 8650752 | tf_op jit(solution)/shard_map/all_gather | solution.py:295
  285.8 373.9 %all-gather.21.cloned.1.call-start = ((), (), s32[]{:S(2)}) async-start(), calls=%async_computation.10 | async-start | bytes 4325376 | tf_op jit(solution)/shard_map/all_gather | solution.py:296
  286.4 544.0 %all-gather.23.cloned.1.call-start = ((), (), s32[]{:S(2)}) async-start(), calls=%async_computation.11 | async-start | bytes 13369344 | tf_op jit(solution)/shard_map/all_gather | solution.py:41
  525.3 143.4 %copy-start.6 = (f32[128,1024]{1,0:T(8,128)}, f32[128,1024]{1,0:T(8,128)S(1)}, u32[]{:S(2)}) copy-start(f32[128,1024]{1,0:T(8,128)S(1)} %get-tuple-element.811) | copy-start | bytes 1572868
  682.9 257.7 %reduce-scatter.7.cloned.1.call-start = ((), (), s32[]{:S(2)}) async-start(), calls=%async_computation.12 | async-start | bytes 1114112 | tf_op jit(solution)/shard_map/reduce_scatter | solution.py:389
  698.7 361.6 %all-gather.27.cloned.1.call-start = ((), (), s32[]{:S(2)}) async-start(), calls=%async_computation.20 | async-start | bytes 13369344 | tf_op jit(solution)/shard_map/all_gather | solution.py:41
  865.0 303.5 %reduce-scatter.9.cloned.1.call-start = ((), (), s32[]{:S(2)}) async-start(), calls=%async_computation.13 | async-start | bytes 1114112 | tf_op jit(solution)/shard_map/reduce_scatter | solution.py:390
  874.3 385.6 %reduce-scatter.13.cloned.1.call-start = ((), (), s32[]{:S(2)}) async-start(), calls=%async_computation.16 | async-start | bytes 8650752 | tf_op jit(solution)/shard_map/reduce_scatter | solution.py:449
  880.1 528.0 %reduce-scatter.17.cloned.1.call-start = ((), (), s32[]{:S(2)}) async-start(), calls=%async_computation.18 | async-start | bytes 8650752 | tf_op jit(solution)/shard_map/reduce_scatter | solution.py:451
  885.9 737.8 %reduce-scatter.15.cloned.1.call-start = ((), (), s32[]{:S(2)}) async-start(), calls=%async_computation.17 | async-start | bytes 17301504 | tf_op jit(solution)/shard_map/reduce_scatter | solution.py:450
  896.2 856.0 %all-reduce.33.cloned.1.call-start = ((), (), s32[]{:S(2)}) async-start(), calls=%async_computation.15 | async-start | bytes 196608 | tf_op jit(solution)/shard_map/psum | solution.py:453
  1147.5 12.7 collective-permute-start.2
  1150.6 12.2 collective-permute-start.3
  1160.2 780.5 %reduce-scatter.11.cloned.1.call-start = ((), (), s32[]{:S(2)}) async-start(), calls=%async_computation.14 | async-start | bytes 17301504 | tf_op jit(solution)/shard_map/reduce_scatter | solution.py:448
  (149 other events, 2048.4 us)
Sparse Core Ops, SparseCore 0:
  10.9 78.5 all-gather.12
  111.1 149.3 all-gather.14
  284.7 168.1 all-gather.24
  455.7 62.3 all-gather.16
  520.8 75.8 all-gather.18
  599.4 60.2 all-gather.20
  683.0 147.2 all-gather.22
  832.6 58.4 reduce-scatter.6
  893.8 166.3 all-gather.26
  1062.4 58.3 reduce-scatter.8
  1123.6 136.2 reduce-scatter.12
  1262.6 145.4 reduce-scatter.16
  1411.0 212.7 reduce-scatter.14
  1629.7 122.3 all-reduce.32
  1754.8 185.7 reduce-scatter.10
where the time goes:
time: 1960 us; the launch traced here: 1950 us
  waiting for transfers between devices  1320 us (67%)
  blocking collectives  180 us (9%)
  other arithmetic  178 us (9%)
  matrix products  143 us (7%)
  local copies, waits for them, and re-layouts  97.9 us (5%)
    all_gather x4, waiting for transfers between devices, carried_in(): everything = jax.tree.map(lambda part: lax.all_gather(part, axis), array)  410 us
    reduce_scatter x1, waiting for transfers between devices, body(): lax.psum_scatter(up_grad, ('ctx', 'wsh'), scatter_dimension=0, tiled=True)  216 us
    reduce_scatter x1, waiting for transfers between devices, body(): lax.psum_scatter(in_grad, ('ctx', 'wsh'), scatter_dimension=0, tiled=True)  189 us
    reduce_scatter x1, waiting for transfers between devices, body(): lax.psum_scatter(down_grad, ('ctx', 'wsh'), scatter_dimension=0, tiled=True)  148 us
    psum x1, waiting for transfers between devices, body(): lax.psum((gain1_part, step_grad, mixer_grads[2], mixer_grads[3], mixer_gr...  128 us
    select_n x64, other arithmetic, hop(): return jax.tree.map(lambda a, b: jnp.where(reached, a, b), new, before)  118 us
    all_gather x1, waiting for transfers between devices, body(): lax.all_gather(mix_in, ('ctx', 'wsh'), axis=0, tiled=True)  76.3 us
    all_gather x1, waiting for transfers between devices, body(): lax.all_gather(mlp_in, ('ctx', 'wsh'), axis=0, tiled=True)  70.3 us
  transfers between devices with their start and end apart: 19, of which 13 were waited for; matrix products, arithmetic and copies ran while one was open for 18% of the time, Pallas kernels for 0%

commit v1 on v0

--- a/solution.py
+++ b/solution.py
@@ -3,6 +3,8 @@
 import jax
 import jax.numpy as jnp
 from jax import lax
+from jax.experimental import pallas as pl
+from jax.experimental.pallas import tpu as pltpu
 from jax.sharding import PartitionSpec as P
 
 MHEADS = 24
@@ -21,37 +23,6 @@
 ROPE_BASE = 10000.0
 NEG_LARGE = -1e30
 HIGHEST = lax.Precision.HIGHEST
-
-
-def with_halo(array, sides, width):
-    for axis, dim in sides:
-        size, length = (lax.axis_size(axis), array.shape[dim])
-        up = [(i, (i + 1) % size) for i in range(size - 1)]
-        down = [(j, i) for i, j in up]
-        last = lax.slice_in_dim(array, length - width, length, axis=dim)
-        leading = lax.slice_in_dim(array, 0, width, axis=dim)
-        before = lax.ppermute(last, axis, up)
-        after = lax.ppermute(leading, axis, down)
-        array = jnp.concatenate([before, array, after], axis=dim)
-    return array
-
-
-def carried_in(array, axis, combine, identity, reverse):
-    size, here = (lax.axis_size(axis), lax.axis_index(axis))
-    everything = jax.tree.map(lambda part: lax.all_gather(part, axis), array)
-    start = jax.tree.map(
-        lambda part, zero: jnp.broadcast_to(jnp.asarray(zero, part.dtype), part.shape),
-        array,
-        identity,
-    )
-
-    def hop(k, before):
-        at = size - 1 - k if reverse else k
-        reached = at > here if reverse else at < here
-        new = combine(before, jax.tree.map(lambda part: part[at], everything))
-        return jax.tree.map(lambda a, b: jnp.where(reached, a, b), new, before)
-
-    return lax.fori_loop(0, size, hop, start)
 
 
 def rms_scale(values, gain_vec):
@@ -141,10 +112,6 @@
     return rms_scale(ssm_out * jax.nn.silu(gate_z), mamba_gain)
 
 
-def chain_combine(earlier, latter):
-    return (earlier[0] * latter[0], latter[0][:, None, None] * earlier[1] + latter[1])
-
-
 def score_block(q_groups, query_pos, key_block, pos_block):
     raw_scores = jnp.einsum(
         "tkgd,skd->kgts", q_groups, key_block, preferred_element_type=jnp.float32
@@ -256,6 +223,54 @@
         grad_keys.reshape(key_count, KV_HEADS * HEAD_DIM),
         grad_values.reshape(key_count, KV_HEADS * HEAD_DIM),
     )
+
+
+def chain_scan(fresh, decays, reverse):
+    dev_count, _, rows, width = fresh.shape
+    spans = 2 * dev_count
+
+    def kernel(fresh_ref, decay_ref, out_ref):
+        state = jnp.zeros((rows, width), jnp.float32)
+        for step in range(spans):
+            at = spans - 1 - step if reverse else step
+            dev, half = (at, 0) if at < dev_count else (spans - 1 - at, 1)
+            out_ref[dev, half] = state.astype(jnp.bfloat16)
+            state = decay_ref[:, at : at + 1] * state + fresh_ref[dev, half].astype(jnp.float32)
+
+    return pl.pallas_call(
+        kernel, out_shape=jax.ShapeDtypeStruct(fresh.shape, jnp.bfloat16), name="chain_scan"
+    )(fresh, decays)
+
+
+def swap(array):
+    return lax.ppermute(array, "wsh", [(0, 1), (1, 0)])
+
+
+def half_pair(values, dev_count, core):
+    tokens, width = values.shape
+    blocks = values.T.reshape(dev_count, 2, width // (2 * dev_count), tokens)
+    own = lax.dynamic_index_in_dim(blocks, core, 1, keepdims=False)
+    other = lax.dynamic_index_in_dim(blocks, 1 - core, 1, keepdims=False)
+    joined = jnp.concatenate([own, swap(other)], axis=-1)
+    return joined.reshape(width // 2, 2 * tokens)
+
+
+def both_cores(values):
+    return jnp.concatenate([values, swap(values)], axis=0)
+
+
+def exchange(array):
+    return lax.all_to_all(array, "ctx", 0, 0, tiled=True)
+
+
+def butterfly_sum(array):
+    array = array + swap(array)
+    size = lax.axis_size("ctx")
+    step = 1
+    while step < size:
+        array = array + lax.ppermute(array, "ctx", [(i, i ^ step) for i in range(size)])
+        step *= 2
+    return array
 
 
 def body(
@@ -276,47 +291,80 @@
     out_grad,
 ):
     residual = inputs[0]
-    row_count = residual.shape[0]
+    row_count, width = residual.shape
     half_rows = row_count // 2
     rim_len = CONV - 1
     q_width = ATT_HEADS * HEAD_DIM
     kv_width = KV_HEADS * HEAD_DIM
     dev_count = lax.axis_size("ctx")
     device = lax.axis_index("ctx")
+    core = lax.axis_index("wsh")
     is_last = device == dev_count - 1
+    state_rows = MHEADS * MHEAD_DIM // dev_count
+    in_rows = mix_in.shape[0]
+    out_rows = mix_out.shape[0]
+    up = [(i, i + 1) for i in range(dev_count - 1)]
+    down = [(j, i) for i, j in up]
     local_pos = token_positions(
         device, dev_count, row_count, jnp.arange(row_count, dtype=jnp.int32)
     )
     key_ids = jnp.arange(row_count * dev_count, dtype=jnp.int32)
     key_pos = token_positions(key_ids // row_count, dev_count, row_count, key_ids % row_count)
-    full_in, full_out, full_up, full_down = (
-        lax.all_gather(mix_in, ("ctx", "wsh"), axis=0, tiled=True),
-        lax.all_gather(mix_out, ("ctx", "wsh"), axis=0, tiled=True),
-        lax.all_gather(mlp_in, ("ctx", "wsh"), axis=0, tiled=True),
-        lax.all_gather(mlp_out, ("ctx", "wsh"), axis=0, tiled=True),
-    )
+    full_in = lax.all_gather(mix_in, ("ctx", "wsh"), axis=0, tiled=True)
+    packed = jnp.concatenate(
+        [jnp.concatenate([mlp_in[:, :FF], mlp_in[:, FF:]], axis=0), mix_out, mlp_out], axis=1
+    )
+    full_in, packed = lax.optimization_barrier((full_in, packed))
+    gathered = lax.all_gather(packed, ("ctx", "wsh"), axis=0)
+    full_gate = gathered[:, :in_rows, :FF].reshape(width, FF)
+    full_upw = gathered[:, in_rows:, :FF].reshape(width, FF)
+    full_out = gathered[:, :, FF : FF + width].reshape(-1, width)
+    full_down = gathered[:, :, FF + width :].reshape(-1, width)
+
     normed1 = rms_scale(residual, norm_gain1).astype(jnp.bfloat16)
-    projected = jnp.dot(normed1, full_in, preferred_element_type=jnp.float32)
+    tail_first = normed1[half_rows - rim_len : half_rows]
+    tail_second = normed1[row_count - rim_len :]
+    rim_first = lax.ppermute(tail_first, "ctx", up)
+    rim_second = jnp.where(is_last, tail_first, lax.ppermute(tail_second, "ctx", down))
+    spare = 16 - 2 * rim_len
+    extended = jnp.concatenate(
+        [normed1, rim_first, rim_second, jnp.zeros((spare, width), jnp.bfloat16)], axis=0
+    )
     step_raw = jnp.dot(normed1, step_proj, preferred_element_type=jnp.float32)
-    gate_z = projected[:, :INNER]
-    conv_in = projected[:, INNER : INNER + CONV_CH]
-    attn_cols = projected[:, INNER + CONV_CH :]
+    step_pair = step_raw.reshape(2, half_rows, MHEADS)
+    early_steps = jax.nn.softplus(step_pair + step_bias[None, None, :])
+    decays = jnp.exp(jnp.sum(early_steps * -jnp.exp(decay_log), axis=1))
+    all_decays = exchange(
+        jnp.broadcast_to(decays.reshape(1, 2 * MHEADS), (dev_count, 2 * MHEADS))
+    ).reshape(dev_count, 2, MHEADS)
+    span_decays = jnp.concatenate([all_decays[:, 0], all_decays[::-1, 1]], axis=0)
+    row_head = (device * state_rows + jnp.arange(state_rows)) // MHEAD_DIM
+    row_pick = (row_head[:, None] == jnp.arange(MHEADS)[None, :]).astype(jnp.float32)
+    row_decays = jnp.dot(row_pick, span_decays.T, precision=HIGHEST)
+    grad_top = out_grad[0]
+    grad_top_b = grad_top.astype(jnp.bfloat16)
+
+    projected = jnp.dot(extended, full_in, preferred_element_type=jnp.float32)
+    gate_z = projected[:row_count, :INNER]
+    conv_all = projected[:, INNER : INNER + CONV_CH]
+    attn_cols = projected[:row_count, INNER + CONV_CH :]
     q_raw = attn_cols[:, :q_width].reshape(row_count, ATT_HEADS, HEAD_DIM)
     k_raw = attn_cols[:, q_width : q_width + kv_width].reshape(row_count, KV_HEADS, HEAD_DIM)
     v_raw = attn_cols[:, q_width + kv_width :]
-    tail_rows = jnp.stack(
-        [conv_in[half_rows - rim_len : half_rows], conv_in[row_count - rim_len :]]
-    )
-    beside_all = with_halo(tail_rows[None], (("ctx", 0),), 1)
-    rim_first = beside_all[0, 0]
-    rim_second = jnp.where(is_last, tail_rows[0], beside_all[2, 1])
     padded = jnp.stack(
         [
-            jnp.concatenate([rim_first, conv_in[:half_rows]], axis=0),
-            jnp.concatenate([rim_second, conv_in[half_rows:]], axis=0),
+            jnp.concatenate(
+                [conv_all[row_count : row_count + rim_len], conv_all[:half_rows]], axis=0
+            ),
+            jnp.concatenate(
+                [
+                    conv_all[row_count + rim_len : row_count + 2 * rim_len],
+                    conv_all[half_rows:row_count],
+                ],
+                axis=0,
+            ),
         ]
     )
-    step_pair = step_raw.reshape(2, half_rows, MHEADS)
 
     def local_parts(padded_one, step_one):
         x_heads, step_size, decay_rate, b_proj, c_proj = mixer_inputs(
@@ -328,67 +376,119 @@
         return (local_out, fresh_state, cumulative, c_proj)
 
     local_out, fresh_state, cumulative, c_proj = jax.vmap(local_parts)(padded, step_pair)
-    decays = jnp.exp(cumulative[:, -1])
-    identity = (
-        jnp.ones((MHEADS,), jnp.float32),
-        jnp.zeros((MHEADS, MHEAD_DIM, STATE), jnp.float32),
-    )
-    rising = carried_in((decays[0], fresh_state[0]), "ctx", chain_combine, identity, False)
-    state_first = rising[1]
-    end_first = decays[0][:, None, None] * state_first + fresh_state[0]
-    lead_second = jnp.where(
-        is_last, decays[1][:, None, None] * end_first + fresh_state[1], fresh_state[1]
-    )
-    falling = carried_in((decays[1], lead_second), "ctx", chain_combine, identity, True)
-    state_second = jnp.where(is_last, end_first, falling[1])
-    states = jnp.stack([state_first, state_second])
+    queries = rope_apply(q_raw, local_pos).astype(jnp.bfloat16)
+    keys_local = rope_apply(k_raw, local_pos).reshape(row_count, kv_width).astype(jnp.bfloat16)
+
+    def to_slices(states):
+        return (
+            states.astype(jnp.bfloat16)
+            .reshape(2, dev_count, state_rows, STATE)
+            .transpose(1, 0, 2, 3)
+            .reshape(dev_count, 2 * state_rows, STATE)
+        )
+
+    def from_slices(slices):
+        return (
+            slices.reshape(dev_count, 2, state_rows, STATE)
+            .transpose(1, 0, 2, 3)
+            .reshape(2, MHEADS, MHEAD_DIM, STATE)
+            .astype(jnp.float32)
+        )
+
+    kv_local = jnp.concatenate([keys_local, v_raw.astype(jnp.bfloat16)], axis=0)
+    arrived = exchange(
+        jnp.concatenate(
+            [
+                to_slices(fresh_state),
+                jnp.broadcast_to(kv_local[None], (dev_count, 2 * row_count, kv_width)),
+            ],
+            axis=1,
+        )
+    )
+    fresh_all = arrived[:, : 2 * state_rows].reshape(dev_count, 2, state_rows, STATE)
+    all_keys = arrived[:, 2 * state_rows : 2 * state_rows + row_count].reshape(-1, kv_width)
+    all_values = arrived[:, 2 * state_rows + row_count :].reshape(-1, kv_width)
+    entering = chain_scan(fresh_all, row_decays, False)
+    states = from_slices(exchange(entering.reshape(dev_count, 2 * state_rows, STATE)))
     ssm_out = (local_out + jax.vmap(carry_term)(c_proj, cumulative, states)).reshape(
         row_count, INNER
     )
     mamba_part = gated_tail(ssm_out, gate_z, mamba_gain)
-    queries = rope_apply(q_raw, local_pos).astype(jnp.bfloat16)
-    keys_local = rope_apply(k_raw, local_pos).reshape(row_count, kv_width).astype(jnp.bfloat16)
-    all_keys, all_values = (
-        lax.all_gather(keys_local, "ctx", axis=0, tiled=True),
-        lax.all_gather(v_raw.astype(jnp.bfloat16), "ctx", axis=0, tiled=True),
-    )
     attn_f32, log_total = attention_forward(queries, all_keys, all_values, local_pos, key_pos)
     joined = jnp.concatenate(
         [mamba_part.astype(jnp.bfloat16), attn_f32.astype(jnp.bfloat16)], axis=1
     )
     middle = residual + jnp.dot(joined, full_out, preferred_element_type=jnp.float32)
     normed2 = rms_scale(middle, norm_gain2).astype(jnp.bfloat16)
-    up_proj = jnp.dot(normed2, full_up, preferred_element_type=jnp.float32)
-    gate_part = up_proj[:, :FF]
-    up_part = up_proj[:, FF:]
+    gate_part = jnp.dot(normed2, full_gate, preferred_element_type=jnp.float32)
+    up_part = jnp.dot(normed2, full_upw, preferred_element_type=jnp.float32)
     activated = (jax.nn.silu(gate_part) * up_part).astype(jnp.bfloat16)
     outputs = middle + jnp.dot(activated, full_down, preferred_element_type=jnp.float32)
-    grad_top = out_grad[0]
-    grad_top_b = grad_top.astype(jnp.bfloat16)
-    down_grad = jnp.dot(activated.T, grad_top_b, preferred_element_type=jnp.float32)
     grad_act = jnp.dot(grad_top_b, full_down.T, preferred_element_type=jnp.float32)
     sigmoid_g = jax.nn.sigmoid(gate_part)
-    grad_gate = grad_act * up_part * sigmoid_g * (1.0 + gate_part * (1.0 - sigmoid_g))
-    grad_up = grad_act * gate_part * sigmoid_g
-    grad_mlp = jnp.concatenate([grad_gate, grad_up], axis=1).astype(jnp.bfloat16)
-    up_grad = jnp.dot(normed2.T, grad_mlp, preferred_element_type=jnp.float32)
-    grad_normed2 = jnp.dot(grad_mlp, full_up.T, preferred_element_type=jnp.float32)
+    grad_gate = (grad_act * up_part * sigmoid_g * (1.0 + gate_part * (1.0 - sigmoid_g))).astype(
+        jnp.bfloat16
+    )
+    grad_up = (grad_act * gate_part * sigmoid_g).astype(jnp.bfloat16)
+    grad_normed2 = jnp.dot(grad_gate, full_gate.T, preferred_element_type=jnp.float32) + jnp.dot(
+        grad_up, full_upw.T, preferred_element_type=jnp.float32
+    )
     unused_two, norm_back2 = jax.vjp(rms_scale, middle, norm_gain2)
     grad_mid_n, gain2_part = norm_back2(grad_normed2)
     grad_middle = grad_top + grad_mid_n
     grad_mid_b = grad_middle.astype(jnp.bfloat16)
-    mixout_grad = jnp.dot(joined.T, grad_mid_b, preferred_element_type=jnp.float32)
+
+    def half_grad(values, grads):
+        return jnp.dot(
+            half_pair(values, dev_count, core),
+            both_cores(grads),
+            preferred_element_type=jnp.float32,
+        ).astype(jnp.bfloat16)
+
+    down_half = half_grad(activated, grad_top_b).reshape(dev_count, out_rows, width)
+    up_half = half_grad(normed2, jnp.concatenate([grad_gate, grad_up], axis=1)).reshape(
+        dev_count, in_rows, 2 * FF
+    )
+    mixout_half = half_grad(joined, grad_mid_b).reshape(dev_count, out_rows, width)
+    grad_pack = jnp.concatenate(
+        [
+            jnp.concatenate([up_half[:, :, :FF], up_half[:, :, FF:]], axis=1),
+            mixout_half,
+            down_half,
+        ],
+        axis=2,
+    ).reshape(dev_count * out_rows, -1)
+    pack_shard = lax.psum_scatter(grad_pack, "ctx", scatter_dimension=0, tiled=True)
+
     grad_joined = jnp.dot(grad_mid_b, full_out.T, preferred_element_type=jnp.float32)
     unused_tail, tail_back = jax.vjp(gated_tail, ssm_out, gate_z, mamba_gain)
     grad_ssm, grad_z, mgain_part = tail_back(grad_joined[:, :INNER])
+    grad_pair = grad_ssm.reshape(2, half_rows, INNER)
+    grad_heads = grad_ssm.reshape(2, half_rows, MHEADS, MHEAD_DIM)
+    own_grads = jnp.einsum(
+        "athp,atn->ahpn",
+        grad_heads * jnp.exp(cumulative)[:, :, :, None],
+        c_proj,
+        precision=HIGHEST,
+    )
     grad_attn = grad_joined[:, INNER:].astype(jnp.bfloat16)
     grad_q, grad_keys, grad_values = attention_backward(
         queries, all_keys, all_values, local_pos, key_pos, log_total, attn_f32, grad_attn
     )
-    keys_back, values_back = (
-        lax.psum_scatter(grad_keys, "ctx", scatter_dimension=0, tiled=True),
-        lax.psum_scatter(grad_values, "ctx", scatter_dimension=0, tiled=True),
-    )
+    kv_grads = jnp.concatenate(
+        [
+            grad_keys.astype(jnp.bfloat16).reshape(dev_count, row_count, kv_width),
+            grad_values.astype(jnp.bfloat16).reshape(dev_count, row_count, kv_width),
+        ],
+        axis=1,
+    )
+    returned = exchange(jnp.concatenate([to_slices(own_grads), kv_grads], axis=1))
+    own_all = returned[:, : 2 * state_rows].reshape(dev_count, 2, state_rows, STATE)
+    kv_back = jnp.sum(returned[:, 2 * state_rows :].astype(jnp.float32), axis=0)
+    keys_back = kv_back[:row_count]
+    values_back = kv_back[row_count:]
+    leaving = chain_scan(own_all, row_decays, True)
+    end_grads = from_slices(exchange(leaving.reshape(dev_count, 2 * state_rows, STATE)))
     unused_q, rope_back_q = jax.vjp(partial(rope_apply, positions=local_pos), q_raw)
     unused_k, rope_back_k = jax.vjp(partial(rope_apply, positions=local_pos), k_raw)
     (grad_q_raw,) = rope_back_q(grad_q)
@@ -405,81 +505,83 @@
         skip_gain,
         states,
     )
-    grad_pair = grad_ssm.reshape(2, half_rows, INNER)
-    first_pass = mixer_back((grad_pair, jnp.zeros_like(states)))
-    own_grads = first_pass[7]
-    back_up = carried_in((decays[1], own_grads[1]), "ctx", chain_combine, identity, False)
-    end_second = back_up[1]
-    start_second = decays[1][:, None, None] * end_second + own_grads[1]
-    lead_first = jnp.where(
-        is_last, decays[0][:, None, None] * start_second + own_grads[0], own_grads[0]
-    )
-    back_down = carried_in((decays[0], lead_first), "ctx", chain_combine, identity, True)
-    end_first_g = jnp.where(is_last, start_second, back_down[1])
-    second_pass = mixer_back((jnp.zeros_like(grad_pair), jnp.stack([end_first_g, end_second])))
-    mixer_grads = jax.tree.map(jnp.add, first_pass, second_pass)
+    mixer_grads = mixer_back((grad_pair, end_grads))
     grad_padded = mixer_grads[0]
-    grad_rims = grad_padded[:, :rim_len]
+    grad_rims = grad_padded[:, :rim_len].reshape(2 * rim_len, CONV_CH)
     grad_conv = grad_padded[:, rim_len:].reshape(row_count, CONV_CH)
-    moved_rims = with_halo(grad_rims[None], (("ctx", 0),), 1)
-    add_first = moved_rims[2, 0] + jnp.where(is_last, grad_rims[1], 0.0)
-    grad_conv = grad_conv.at[half_rows - rim_len : half_rows].add(add_first)
-    grad_conv = grad_conv.at[row_count - rim_len :].add(moved_rims[0, 1])
     grad_proj = jnp.concatenate(
         [
-            grad_z,
-            grad_conv,
-            grad_q_raw.reshape(row_count, q_width),
-            grad_k_raw.reshape(row_count, kv_width),
-            values_back,
+            jnp.concatenate(
+                [
+                    grad_z,
+                    grad_conv,
+                    grad_q_raw.reshape(row_count, q_width),
+                    grad_k_raw.reshape(row_count, kv_width),
+                    values_back,
+                ],
+                axis=1,
+            ).astype(jnp.bfloat16),
+            jnp.pad(
+                grad_rims.astype(jnp.bfloat16), ((0, spare), (INNER, q_width + 2 * kv_width))
+            ),
         ],
-        axis=1,
-    ).astype(jnp.bfloat16)
+        axis=0,
+    )
+    in_half = half_grad(extended, grad_proj)
+    in_shard = lax.psum_scatter(in_half, "ctx", scatter_dimension=0, tiled=True)
     grad_step = mixer_grads[1].reshape(row_count, MHEADS).astype(jnp.bfloat16)
-    in_grad = jnp.dot(normed1.T, grad_proj, preferred_element_type=jnp.float32)
-    step_grad = jnp.dot(normed1.T, grad_step, preferred_element_type=jnp.float32)
-    grad_normed1 = jnp.dot(grad_proj, full_in.T, preferred_element_type=jnp.float32) + jnp.dot(
-        grad_step, step_proj.T, preferred_element_type=jnp.float32
+    step_grad = jnp.dot(grad_step.T, normed1, preferred_element_type=jnp.float32)
+    grad_ext = jnp.dot(grad_proj, full_in.T, preferred_element_type=jnp.float32)
+    back_first = grad_ext[row_count : row_count + rim_len]
+    back_second = grad_ext[row_count + rim_len : row_count + 2 * rim_len]
+    add_first = lax.ppermute(back_first, "ctx", down) + jnp.where(is_last, back_second, 0.0)
+    add_second = lax.ppermute(back_second, "ctx", up)
+    fill = jnp.zeros((half_rows - rim_len, width), jnp.float32)
+    grad_normed1 = (
+        grad_ext[:row_count]
+        + jnp.concatenate([fill, add_first, fill, add_second], axis=0)
+        + jnp.dot(grad_step, step_proj.T, preferred_element_type=jnp.float32)
     )
     unused_one, norm_back1 = jax.vjp(rms_scale, residual, norm_gain1)
     grad_res_n, gain1_part = norm_back1(grad_normed1)
     input_grad = grad_middle + grad_res_n
-    in_shard, out_shard, up_shard, down_shard = (
-        lax.psum_scatter(in_grad, ("ctx", "wsh"), scatter_dimension=0, tiled=True),
-        lax.psum_scatter(mixout_grad, ("ctx", "wsh"), scatter_dimension=0, tiled=True),
-        lax.psum_scatter(up_grad, ("ctx", "wsh"), scatter_dimension=0, tiled=True),
-        lax.psum_scatter(down_grad, ("ctx", "wsh"), scatter_dimension=0, tiled=True),
-    )
-    small_sums = lax.psum(
-        (
-            gain1_part,
-            step_grad,
-            mixer_grads[2],
-            mixer_grads[3],
-            mixer_grads[4],
-            mixer_grads[5],
-            mixer_grads[6],
-            mgain_part,
-            gain2_part,
-        ),
-        ("ctx", "wsh"),
-    )
+    parts = (
+        gain1_part,
+        step_grad,
+        mixer_grads[2],
+        mixer_grads[3],
+        mgain_part,
+        gain2_part,
+        mixer_grads[4],
+        mixer_grads[5],
+        mixer_grads[6],
+    )
+    flat = jnp.concatenate([part.reshape(-1) for part in parts])
+    total_len = flat.shape[0]
+    summed = butterfly_sum(jnp.pad(flat, (0, -total_len % 1024)).reshape(-1, 128)).reshape(-1)
+    sums = []
+    start = 0
+    for part in parts:
+        sums.append(summed[start : start + part.size].reshape(part.shape))
+        start += part.size
+    pack_f32 = pack_shard.astype(jnp.float32)
+    up_shard = jnp.concatenate([pack_f32[:in_rows, :FF], pack_f32[in_rows:, :FF]], axis=1)
     return (
         outputs[None],
         input_grad[None],
-        small_sums[0],
-        in_shard,
-        small_sums[1],
-        small_sums[2],
-        small_sums[3],
-        small_sums[4],
-        small_sums[5],
-        small_sums[6],
-        small_sums[7],
-        out_shard,
-        small_sums[8],
+        sums[0],
+        in_shard.astype(jnp.float32),
+        sums[1].T,
+        sums[2],
+        sums[3],
+        sums[6],
+        sums[7],
+        sums[8],
+        sums[4],
+        pack_f32[:, FF : FF + width],
+        sums[5],
         up_shard,
-        down_shard,
+        pack_f32[:, FF + width :],
     )
 
 

time: 1960 us -> 730 us (0.37)
  waiting for transfers between devices: 1320 us -> 393 us
  blocking collectives: 180 us -> 0 us
  other arithmetic: 178 us -> 56 us
  matrix products: 143 us -> 96.6 us
  starting transfers between devices: 11.9 us -> 46.7 us
    all_gather x8 -> x2, waiting for transfers between devices: 614 us -> 78.7 us  [the longest x1 78.7 us: body(): full_in = lax.all_gather(mix_in, ('ctx', 'wsh'), axis=0, tiled=True)]
    reduce_scatter x6 -> x2, waiting for transfers between devices: 573 us -> 165 us  [the longest x1 164 us: body(): lax.psum_scatter(grad_pack, 'ctx', scatter_dimension=0, tiled=True)]
    all_gather x4 -> x0, blocking collectives: 134 us -> none  [the longest x2 49.3 us: carried_in(): everything = jax.tree.map(lambda part: lax.all_gather(part, axis), array)]
    psum x1 -> x0, waiting for transfers between devices: 128 us -> none  [body(): lax.psum((gain1_part, step_grad, mixer_grads[2], mixer_grads[3], mixer_gr...]
    select_n x67 -> x1, other arithmetic: 123 us -> 0.01 us  [body(): row_head = (device * state_rows + jnp.arange(state_rows)) // MHEAD_DIM]
    all_to_all x0 -> x5, waiting for transfers between devices: none -> 122 us  [exchange(): return lax.all_to_all(array, 'ctx', 0, 0, tiled=True)]
    psum x1 -> x0, blocking collectives: 45.9 us -> none  [body(): lax.psum((gain1_part, step_grad, mixer_grads[2], mixer_grads[3], mixer_gr...]
    mul x65 -> x0, local copies, waits for them, and re-layouts: 33 us -> none  [the longest x64 33 us: chain_combine(): latter[0][:, None, None] * earlier[1] + latter[1]]
  transfers between devices with their start and end apart: 19 -> 26, of which waited for: 13 -> 14; matrix products, arithmetic and copies ran while one was open for 18% -> 22% of each run, Pallas kernels for 0% -> 0%
where the time goes in v1:
time: 730 us; the launch traced here: 717 us
  waiting for transfers between devices  393 us (54%)
  local copies, waits for them, and re-layouts  103 us (14%)
  matrix products  96.6 us (13%)
  other arithmetic  56 us (8%)
  starting transfers between devices  46.7 us (6%)
  between operations  16.3 us (2%)
    reduce_scatter x1, waiting for transfers between devices, body(): lax.psum_scatter(grad_pack, 'ctx', scatter_dimension=0, tiled=True)  164 us
    all_to_all x5, waiting for transfers between devices, exchange(): return lax.all_to_all(array, 'ctx', 0, 0, tiled=True)  122 us
    all_gather x1, waiting for transfers between devices, body(): full_in = lax.all_gather(mix_in, ('ctx', 'wsh'), axis=0, tiled=True)  78.7 us
    all_to_all x5, starting transfers between devices, exchange(): return lax.all_to_all(array, 'ctx', 0, 0, tiled=True)  26.3 us
    unnamed x272, local copies, waits for them, and re-layouts  18.6 us
    ppermute x4, waiting for transfers between devices, butterfly_sum(): lax.ppermute(array, 'ctx', [(i, i ^ step) for i in range(size)])  17.6 us
    dot_general x4, matrix products, half_grad(): jnp.dot(half_pair(values, dev_count, core), both_cores(grads), preferred_...  15 us
  transfers between devices with their start and end apart: 26, of which 14 were waited for; matrix products, arithmetic and copies ran while one was open for 22% of the time, Pallas kernels for 0%

profile of v1, /device:TPU:13, one launch (start us, length us, event | category | flops | bytes accessed | tf_op | source)
XLA Modules:
  0.0 717.1 jit_solution(174566265958841273)
XLA Ops:
  10.8 78.7 %all-gather.4.cloned.1.call-done = bf16[1024,4096]{1,0:T(8,128)(2,1)} async-done(((bf16[32,4096]{1,0:T(8,128)(2,1)}), bf16[1024,4096]{1,0:T(8,128)(2,1)}) %all-gather.4.cloned.1.call-update) | async-done | bytes 8388624 | tf_op jit(solution)/shard_map/all_gather | solution.py:313
  91.6 4.1 all-to-all-start.1
  100.7 4.6 collective-permute-start
  106.8 4.9 fusion.192
  121.8 6.2 all-to-all-start
  138.0 64.9 %all-to-all-done = bf16[16,448,128]{2,1,0:T(8,128)(2,1)} async-done(((bf16[16,448,128]{2,1,0:T(8,128)(2,1)}), bf16[16,448,128]{2,1,0:T(8,128)(2,1)}, u32[]{:S(2)}, u32[]{:S(2)}) %all-to-all-start) | async-done | bytes 1835040 | tf_op jit(solution)/shard_map/all_to_all | solution.py:263
  210.6 7.2 %all-to-all-start.2 = ((bf16[16,192,128]{2,1,0:T(8,128)(2,1)}), bf16[16,192,128]{2,1,0:T(8,128)(2,1)S(1)}, u32[]{:S(2)}, u32[]{:S(2)}) async-start(bf16[16,192,128]{2,1,0:T(8,128)(2,1)} %bitcast.334), calls=%async_computation.2 | async-start | bytes 1572864 | tf_op jit(solution)/shard_map/all_to_all | solution.py:263
  232.2 14.9 %all-to-all-done.2 = bf16[16,192,128]{2,1,0:T(8,128)(2,1)S(1)} async-done(((bf16[16,192,128]{2,1,0:T(8,128)(2,1)}), bf16[16,192,128]{2,1,0:T(8,128)(2,1)S(1)}, u32[]{:S(2)}, u32[]{:S(2)}) %all-to-all-start.2) | async-done | bytes 786464 | tf_op jit(solution)/shard_map/all_to_all | solution.py:263
  251.0 4.3 fusion.22
  262.2 4.2 fusion.205
  266.4 4.2 copy-done.6
  292.8 6.3 fusion.6
  299.1 5.2 fusion.1
  319.2 4.6 all-to-all-start.3
  329.4 5.5 fusion.67
  334.9 31.7 %all-to-all-done.3 = bf16[16,448,128]{2,1,0:T(8,128)(2,1)} async-done(((bf16[16,448,128]{2,1,0:T(8,128)(2,1)}), bf16[16,448,128]{2,1,0:T(8,128)(2,1)}, u32[]{:S(2)}, u32[]{:S(2)}) %all-to-all-start.3) | async-done | bytes 1835040 | tf_op jit(solution)/shard_map/all_to_all | solution.py:263
  371.3 4.2 all-to-all-start.4
  384.3 10.2 %all-to-all-done.4 = bf16[16,192,128]{2,1,0:T(8,128)(2,1)} async-done(((bf16[16,192,128]{2,1,0:T(8,128)(2,1)}), bf16[16,192,128]{2,1,0:T(8,128)(2,1)}, u32[]{:S(2)}, u32[]{:S(2)}) %all-to-all-start.4) | async-done | bytes 786464 | tf_op jit(solution)/shard_map/all_to_all | solution.py:263
  424.1 5.9 convolution_convert_fusion.1
  459.3 4.0 copy.385
  488.1 6.7 fusion.193
  511.8 11.4 %collective-permute-done.5 = f32[296,128]{1,0:T(8,128)S(1)} collective-permute-done((f32[296,128]{1,0:T(8,128)S(1)}, f32[296,128]{1,0:T(8,128)S(1)}, u32[]{:S(2)}, u32[]{:S(2)}) %collective-permute-start.5) | collective-permute-done | bytes 151584 | tf_op jit(solution)/shard_map/ppermute | solution.py:271
  523.3 4.3 fusion.49
  542.9 164.5 %reduce-scatter.5.cloned.1.call-done = bf16[64,4096]{1,0:T(8,128)(2,1)} async-done(((bf16[1024,4096]{1,0:T(8,128)(2,1)}), bf16[64,4096]{1,0:T(8,128)(2,1)}) %reduce-scatter.5.cloned.1.call-update) | async-done | bytes 524304 | tf_op jit(solution)/shard_map/reduce_scatter | solution.py:461
  (524 shorter events, 238.2 us)
Async XLA Ops:
  7.2 82.3 %all-gather.4.cloned.1.call-start = ((), (), s32[]{:S(2)}) async-start(), calls=%async_computation.7 | async-start | bytes 8650752 | tf_op jit(solution)/shard_map/all_gather | solution.py:313
  8.0 254.2 %all-gather.6.cloned.1.call-start = ((), (), s32[]{:S(2)}) async-start(), calls=%async_computation.10 | async-start | bytes 17301504 | tf_op jit(solution)/shard_map/all_gather | solution.py:318
  91.6 30.1 %all-to-all-start.1 = ((f32[16,1,48]{2,1,0:T(1,128)}), f32[16,1,48]{2,1,0:T(1,128)}, u32[]{:S(2)}, u32[]{:S(2)}) async-start(f32[16,1,48]{2,1,0:T(1,128)} %broadcast_in_dim.131), calls=%async_computation.1 | async-start | bytes 16384 | tf_op jit(solution)/shard_map/all_to_all | solution.py:263
  95.9 4.8 collective-permute-start.1
  100.7 6.1 collective-permute-start
  121.8 81.2 %all-to-all-start = ((bf16[16,448,128]{2,1,0:T(8,128)(2,1)}), bf16[16,448,128]{2,1,0:T(8,128)(2,1)}, u32[]{:S(2)}, u32[]{:S(2)}) async-start(bf16[16,448,128]{2,1,0:T(8,128)(2,1)} %pad_maximum_fusion.2), calls=%async_computation | async-start | bytes 3670016 | tf_op jit(solution)/shard_map/all_to_all | solution.py:263
  210.6 36.6 %all-to-all-start.2 = ((bf16[16,192,128]{2,1,0:T(8,128)(2,1)}), bf16[16,192,128]{2,1,0:T(8,128)(2,1)S(1)}, u32[]{:S(2)}, u32[]{:S(2)}) async-start(bf16[16,192,128]{2,1,0:T(8,128)(2,1)} %bitcast.334), calls=%async_computation.2 | async-start | bytes 1572864 | tf_op jit(solution)/shard_map/all_to_all | solution.py:263
  319.2 47.4 %all-to-all-start.3 = ((bf16[16,448,128]{2,1,0:T(8,128)(2,1)}), bf16[16,448,128]{2,1,0:T(8,128)(2,1)}, u32[]{:S(2)}, u32[]{:S(2)}) async-start(bf16[16,448,128]{2,1,0:T(8,128)(2,1)} %pad_maximum_fusion.3), calls=%async_computation.3 | async-start | bytes 3670016 | tf_op jit(solution)/shard_map/all_to_all | solution.py:263
  371.3 23.2 %all-to-all-start.4 = ((bf16[16,192,128]{2,1,0:T(8,128)(2,1)}), bf16[16,192,128]{2,1,0:T(8,128)(2,1)}, u32[]{:S(2)}, u32[]{:S(2)}) async-start(bf16[16,192,128]{2,1,0:T(8,128)(2,1)} %bitcast.333), calls=%async_computation.4 | async-start | bytes 1572864 | tf_op jit(solution)/shard_map/all_to_all | solution.py:263
  375.5 165.7 %reduce-scatter.3.cloned.1.call-start = ((), (), s32[]{:S(2)}) async-start(), calls=%async_computation.8 | async-start | bytes 4456448 | tf_op jit(solution)/shard_map/reduce_scatter | solution.py:531
  418.7 5.4 collective-permute-start.10
  430.1 277.3 %reduce-scatter.5.cloned.1.call-start = ((), (), s32[]{:S(2)}) async-start(), calls=%async_computation.9 | async-start | bytes 8912896 | tf_op jit(solution)/shard_map/reduce_scatter | solution.py:461
  432.2 23.9 %collective-permute-start.16 = (bf16[128,1024]{1,0:T(8,128)(2,1)}, bf16[128,1024]{1,0:T(8,128)(2,1)}, u32[]{:S(2)}, u32[]{:S(2)}) collective-permute-start(bf16[128,1024]{1,0:T(8,128)(2,1)} %bitcast_convert_fusion), channel_id=1, source_target_pairs={{0,1},{1,0},{2,3},{3,2},{4,5},{5,4},{6,7},{7,6},{8,9},{9,8},{10,11... | collective-permute-start | bytes 786440 | tf_op jit(solution)/shard_map/ppermute | solution.py:246
  434.7 28.6 %collective-permute-start.12 = (bf16[128,4096]{1,0:T(8,128)(2,1)}, bf16[128,4096]{1,0:T(8,128)(2,1)}, u32[]{:S(2)}, u32[]{:S(2)}) collective-permute-start(bf16[128,4096]{1,0:T(8,128)(2,1)} %pad_maximum_fusion.5), channel_id=1, source_target_pairs={{0,1},{1,0},{2,3},{3,2},{4,5},{5,4},{6,7},{7,6},{8,9},{9,8},{10,11... | collective-permute-start | bytes 3145736 | tf_op jit(solution)/shard_map/ppermute | solution.py:246
  439.7 8.8 %collective-permute-start.13 = (bf16[16,64,128]{2,1,0:T(8,128)(2,1)}, bf16[16,64,128]{2,1,0:T(8,128)(2,1)}, u32[]{:S(2)}, u32[]{:S(2)}) collective-permute-start(bf16[16,64,128]{2,1,0:T(8,128)(2,1)} %get-tuple-element.165), channel_id=1, source_target_pairs={{0,1},{1,0},{2,3},{3,2},{4,5},{5,4},{6,7},{7,6},{8,9},{9,8},{10,11... | collective-permute-start | bytes 786440 | tf_op jit(solution)/shard_map/ppermute | solution.py:246
  439.9 9.0 %collective-permute-start.14 = (bf16[128,1024]{1,0:T(8,128)(2,1)S(1)}, bf16[128,1024]{1,0:T(8,128)(2,1)}, u32[]{:S(2)}, u32[]{:S(2)}) collective-permute-start(bf16[128,1024]{1,0:T(8,128)(2,1)S(1)} %copy-done.35), channel_id=1, source_target_pairs={{0,1},{1,0},{2,3},{3,2},{4,5},{5,4},{6,7},{7,6},{8,9},{9,8},{10,11... | collective-permute-start | bytes 786440 | tf_op jit(solution)/shard_map/ppermute | solution.py:246
  446.7 9.3 %collective-permute-start.15 = (bf16[16,64,128]{2,1,0:T(8,128)(2,1)}, bf16[16,64,128]{2,1,0:T(8,128)(2,1)}, u32[]{:S(2)}, u32[]{:S(2)}) collective-permute-start(bf16[16,64,128]{2,1,0:T(8,128)(2,1)} %get-tuple-element.167), channel_id=1, source_target_pairs={{0,1},{1,0},{2,3},{3,2},{4,5},{5,4},{6,7},{7,6},{8,9},{9,8},{10,11... | collective-permute-start | bytes 786440 | tf_op jit(solution)/shard_map/ppermute | solution.py:246
  448.5 14.7 %collective-permute-start.11 = (bf16[16,32,128]{2,1,0:T(8,128)(2,1)}, bf16[16,32,128]{2,1,0:T(8,128)(2,1)}, u32[]{:S(2)}, u32[]{:S(2)}) collective-permute-start(bf16[16,32,128]{2,1,0:T(8,128)(2,1)} %get-tuple-element.175), channel_id=1, source_target_pairs={{0,1},{1,0},{2,3},{3,2},{4,5},{5,4},{6,7},{7,6},{8,9},{9,8},{10,11... | collective-permute-start | bytes 393224 | tf_op jit(solution)/shard_map/ppermute | solution.py:246
  494.9 6.7 collective-permute-start.2
  501.6 5.9 collective-permute-start.3
  511.7 11.4 %collective-permute-start.5 = (f32[296,128]{1,0:T(8,128)S(1)}, f32[296,128]{1,0:T(8,128)S(1)}, u32[]{:S(2)}, u32[]{:S(2)}) collective-permute-start(f32[296,128]{1,0:T(8,128)S(1)} %fusion.188), channel_id=1, source_target_pairs={{0,2},{2,0},{4,6},{6,4},{8,10},{10,8},{12,14},{14,12},{16,18},{18,... | collective-permute-start | bytes 454664 | tf_op jit(solution)/shard_map/ppermute | solution.py:271
  523.2 4.9 collective-permute-start.6
  528.1 4.1 collective-permute-start.7
  532.2 5.2 collective-permute-start.8
  (135 other events, 1520.9 us)
Sparse Core Ops, SparseCore 0:
  10.9 78.5 all-gather.3
  93.0 149.3 all-gather.5
  430.2 95.8 reduce-scatter.2
  528.3 179.0 reduce-scatter.4
